TPU v7x, 128 devices: a whole 4x4x4 slice. The times are simulated.
128 devices in a mesh: ex: 16 (over z, y), feat: 8 (over x, core).
Axes of the slice: x: 4, y: 4, z: 4, core: 2. Of those that a mesh axis runs over, the one named last changes fastest.
Arguments:
- tiles: bfloat16 [16, 8, 384, 128, 128], P('ex', 'feat'), may hold values from -0.5 to 0.5
- row_index: int32 [16, 8, 384], P('ex', 'feat'), may hold values from 0 to 2047
- col_index: int32 [16, 8, 384], P('ex', 'feat'), may hold values from 0 to 4095
- weights: bfloat16 [32768, 128], P('feat'), may hold values from -6 to 6
- val_grad: float32 [32768, 128], P('feat'), may hold values from -6 to 6
- field_map: int32 [32768, 128], P('feat'), may hold values from 0 to 63
- field_lambda: float32 [64], replicated, may hold values from 0.05 to 2
Outputs:
- solution: float32 [32768, 128], P(('feat', 'ex'))
- hypergrad: float32 [64], replicated
Inputs may be any that keep to these rules, and one draw needn't show every extreme that they name: `row_index`: local row tile of a stored tile within its device's 2048 row tiles. `col_index`: local column tile of a stored tile within its device's 4096 column tiles.
All inputs are finite; a program needn't handle non-finite values.
Results may differ from a plain program's by a relative error of at most 0.0021.
Values may be sent and summed in bfloat16 or wider, within the bound.
A program may use at most 128 MiB of HBM per device.

v0:
```python
import math

import jax
import jax.numpy as jnp
from jax import lax
from jax.sharding import PartitionSpec as P

RT_DEV = 2048
ITERS = 3


def on_device(tiles, row_index, col_index, weights, val_grad, field_map, field_lambda):
    tile_count = tiles.shape[2]
    tile_width = tiles.shape[3]
    tile_stack = tiles.reshape(tile_count, tile_width, tile_width)
    row_ids = row_index.reshape(tile_count)
    col_ids = col_index.reshape(tile_count)
    segment = weights.shape[0]
    share_len = segment // lax.axis_size("ex")
    offset = lax.axis_index("ex") * share_len
    field_count = field_lambda.shape[0]
    labels = jnp.arange(field_count, dtype=jnp.int32)
    norm_scale = 1.0 / math.sqrt(segment * tile_width * lax.axis_size("feat") // field_count)

    def own_part(vector):
        return lax.dynamic_slice_in_dim(vector, offset, share_len, 0)

    def forward(vec_b):
        pieces = jnp.take(vec_b, col_ids, axis=0)
        products = jnp.einsum("tij,tj->ti", tile_stack, pieces, preferred_element_type=jnp.float32)
        partial_rows = jnp.zeros((RT_DEV, tile_width), jnp.float32).at[row_ids].add(products)
        return lax.psum(partial_rows, "feat")

    def lookup(field_block):
        matches = field_block[..., None] == labels
        return jnp.sum(jnp.where(matches, field_lambda, 0.0), axis=-1)

    margin = forward(weights)
    prob = jax.nn.sigmoid(margin)
    curv_weight = prob * (1.0 - prob)
    count = field_map.shape[0]
    block_rows = math.gcd(count, 256)
    lam_part = lax.map(lookup, field_map.reshape(-1, block_rows, tile_width)).reshape(
        count, tile_width
    )
    residual = val_grad

    def local(vector):
        return own_part(vector)

    direction = residual
    solution = jnp.zeros_like(residual)
    dir_b = val_grad.astype(jnp.bfloat16)
    mine = local(residual)
    norm_now = lax.psum(jnp.sum(mine * mine), ("ex", "feat"))
    for step in range(ITERS):
        rows_sum = forward(dir_b)
        scaled_part = (curv_weight * rows_sum).astype(jnp.bfloat16)
        backward_pieces = jnp.take(scaled_part, row_ids, axis=0)
        backward_products = jnp.einsum(
            "tij,ti->tj", tile_stack, backward_pieces, preferred_element_type=jnp.float32
        )
        partial_feat = (
            jnp.zeros((segment, tile_width), jnp.float32).at[col_ids].add(backward_products)
        )
        image = lax.psum(partial_feat, "ex") + lam_part * direction
        own_dir = local(direction)
        own_image = local(image)
        curv_sum = lax.psum(jnp.sum(own_dir * own_image), ("ex", "feat"))
        step_size = norm_now / curv_sum
        solution = solution + step_size * direction
        residual = residual - step_size * image
        if step + 1 < ITERS:
            own_res = local(residual)
            next_norm = lax.psum(jnp.sum(own_res * own_res), ("ex", "feat"))
        if step + 1 < ITERS:
            direction = residual + next_norm / norm_now * direction
            norm_now = next_norm
            dir_b = direction.astype(jnp.bfloat16)
    own_solution = local(solution)
    own_terms = own_solution * own_part(weights).astype(jnp.float32)
    own_fields = own_part(field_map)
    share_block = math.gcd(share_len, 256)

    def field_sums(element):
        term_block, field_block = element
        matches = field_block[..., None] == labels
        return jnp.sum(jnp.where(matches, term_block[..., None], 0.0), axis=(0, 1))

    per_block = lax.map(
        field_sums,
        (
            own_terms.reshape(-1, share_block, tile_width),
            own_fields.reshape(-1, share_block, tile_width),
        ),
    )
    totals = lax.psum(jnp.sum(per_block, axis=0), ("ex", "feat"))
    hypergrad = -field_lambda * totals * norm_scale
    return (own_solution, hypergrad)


def solution(mesh):
    return jax.shard_map(
        on_device,
        mesh=mesh,
        in_specs=(
            P("ex", "feat", None, None, None),
            P("ex", "feat", None),
            P("ex", "feat", None),
            P("feat", None),
            P("feat", None),
            P("feat", None),
            P(),
        ),
        out_specs=(P(("feat", "ex"), None), P()),
        check_vma=False,
    )
```

profile of v0, /device:TPU:1, one launch (start us, length us, event | category | flops | bytes accessed | tf_op | source)
XLA Modules:
  0.0 994.5 jit_solution(16957785030988315214)
XLA Ops:
  12.9 10.9 %fusion.14 = f32[384,1,128]{2,1,0:T(1,128)S(1)} fusion(bf16[1,1,384,128,128]{4,3,2,1,0:T(8,128)(2,1)} %param.13, bf16[384,128,1]{1,0,2:T(8,128)(2,1)S(1)} %get-tuple-element.77), kind=kOutput, calls=%fused_computation.31 | convolution fusion | flops 12582912 | bytes 12877824 | tf_op jit(solution)/shard_map/tij,tj->ti/dot_general | solution.py:30
  23.8 6.6 fusion.12
  36.4 66.9 %all-reduce.19.cloned.1.call-done = (f32[2048,128]{1,0:T(8,128)}, f32[2048,128]{1,0:T(8,128)}) async-done(((f32[2048,128]{1,0:T(8,128)}, f32[2048,128]{1,0:T(8,128)}), (f32[2048,128]{1,0:T(8,128)}, f32[2048,128]{1,0:T(8,128)})) %all-reduce.19.cloned.1.call-update) | async-done | bytes 2097168 | tf_op jit(solution)/shard_map/psum | solution.py:32
  106.7 6.4 fusion.10
  113.1 3.2 scatter_custom_fusion.2
  116.4 71.8 %while.3 = (s32[]{:T(128)}, f32[16,256,128]{2,1,0:T(8,128)}, s32[16,256,128]{2,1,0:T(8,128)}, f32[64]{0:T(128)S(1)}, s32[]{:T(128)}) while((s32[]{:T(128)}, f32[16,256,128]{2,1,0:T(8,128)}, s32[16,256,128]{2,1,0:T(8,128)}, f32[64]{0:T(128)S(1)}, s32[]{:T(128)}) %tuple.52), condition=%wide.region_10.13_spmd.clone, body=%wide.region_8.12_spmd.clone.sunk | while | flops 6258690 | bytes 787265 | solution.py:43
  117.5 2.9 select_reduce_fusion.3
  121.9 2.9 select_reduce_fusion.3
  126.4 2.9 select_reduce_fusion.3
  130.9 2.9 select_reduce_fusion.3
  188.2 19.2 %all-reduce.9.cloned.1.call-done = f32[4096,128]{1,0:T(8,128)} async-done(((f32[4096,128]{1,0:T(8,128)}), f32[4096,128]{1,0:T(8,128)}) %all-reduce.9.cloned.1.call-update) | async-done | bytes 2097168 | tf_op jit(solution)/shard_map/psum | solution.py:66
  207.4 3.9 multiply_add_fusion.3
  212.8 65.3 %all-reduce = (f32[]{:T(128)}, f32[]{:T(128)}) all-reduce(f32[]{:T(128)} %get-tuple-element.58, f32[]{:T(128)} %get-tuple-element.57), channel_id=1, replica_groups=mesh['ex'=16,'feat'=8] {'ex','feat'}, use_global_device_ids=true, to_apply=%region_1.2 | all-reduce | flops 2 | bytes 16 | tf_op jit(solution)/shard_map/psum | solution.py:55
  279.5 3.1 multiply_subtract_fusion.1
  284.2 62.8 %psum.103 = f32[]{:T(128)} all-reduce(f32[]{:T(128)} %multiply_reduce_fusion.2), channel_id=1, replica_groups=mesh['ex'=16,'feat'=8] {'ex','feat'}, use_global_device_ids=true, to_apply=%region_14.17 | all-reduce | flops 1 | bytes 8 | tf_op jit(solution)/shard_map/psum | solution.py:75
  348.3 3.2 fusion.42
  353.0 9.5 fusion.8
  365.4 57.4 %all-reduce.11.cloned.1.call-done = f32[2048,128]{1,0:T(8,128)} async-done(((f32[2048,128]{1,0:T(8,128)}), f32[2048,128]{1,0:T(8,128)}) %all-reduce.11.cloned.1.call-update) | async-done | bytes 1048592 | tf_op jit(solution)/shard_map/psum | solution.py:32
  427.7 6.4 fusion.6
  434.0 3.3 scatter_custom_fusion.4
  437.4 90.8 %all-reduce.13.cloned.1.call-done = f32[4096,128]{1,0:T(8,128)} async-done(((f32[4096,128]{1,0:T(8,128)}), f32[4096,128]{1,0:T(8,128)}) %all-reduce.13.cloned.1.call-update) | async-done | bytes 2097168 | tf_op jit(solution)/shard_map/psum | solution.py:66
  528.2 3.2 multiply_add_fusion.1
  534.2 65.4 %psum.106 = f32[]{:T(128)} all-reduce(f32[]{:T(128)} %multiply_reduce_fusion.1), channel_id=1, replica_groups=mesh['ex'=16,'feat'=8] {'ex','feat'}, use_global_device_ids=true, to_apply=%region_20.23 | all-reduce | flops 1 | bytes 8 | tf_op jit(solution)/shard_map/psum | solution.py:69
  605.3 62.8 %psum.107 = f32[]{:T(128)} all-reduce(f32[]{:T(128)} %multiply_reduce_fusion), channel_id=1, replica_groups=mesh['ex'=16,'feat'=8] {'ex','feat'}, use_global_device_ids=true, to_apply=%region_22.25 | all-reduce | flops 1 | bytes 8 | tf_op jit(solution)/shard_map/psum | solution.py:75
  669.4 4.3 fusion.41
  676.4 9.5 fusion.4
  688.7 57.5 %all-reduce.15.cloned.1.call-done = f32[2048,128]{1,0:T(8,128)} async-done(((f32[2048,128]{1,0:T(8,128)}), f32[2048,128]{1,0:T(8,128)}) %all-reduce.15.cloned.1.call-update) | async-done | bytes 1048592 | tf_op jit(solution)/shard_map/psum | solution.py:32
  751.0 6.4 fusion.2
  757.4 3.3 scatter_custom_fusion.6
  760.7 90.9 %all-reduce.17.cloned.1.call-done = f32[4096,128]{1,0:T(8,128)} async-done(((f32[4096,128]{1,0:T(8,128)}), f32[4096,128]{1,0:T(8,128)}) %all-reduce.17.cloned.1.call-update) | async-done | bytes 2097168 | tf_op jit(solution)/shard_map/psum | solution.py:66
  854.2 65.4 %psum.110 = f32[]{:T(128)} all-reduce(f32[]{:T(128)} %fusion.38), channel_id=1, replica_groups=mesh['ex'=16,'feat'=8] {'ex','feat'}, use_global_device_ids=true, to_apply=%region_28.31 | all-reduce | flops 1 | bytes 8 | tf_op jit(solution)/shard_map/psum | solution.py:69
  924.2 62.6 %psum.111 = f32[64]{0:T(128)S(1)} all-reduce(f32[64]{0:T(128)S(1)} %select_reduce_fusion.1), channel_id=1, replica_groups=mesh['ex'=16,'feat'=8] {'ex','feat'}, use_global_device_ids=true, to_apply=%region_30.33 | all-reduce | flops 64 | bytes 512 | tf_op jit(solution)/shard_map/psum | solution.py:97
  (115 shorter events, 111.5 us)
Async XLA Ops:
  7.2 4.1 copy-start.5
  7.2 96.1 %all-reduce.19.cloned.1.call-start = ((), (), s32[]{:S(2)}) async-start(), calls=%async_computation.5 | async-start | bytes 4194304 | tf_op jit(solution)/shard_map/psum | solution.py:32
  8.0 4.7 copy-start.7
  8.0 4.7 copy-start.8
  12.9 10.9 %copy-start = (bf16[1,1,384,128,128]{4,3,2,1,0:T(8,128)(2,1)S(1)}, bf16[1,1,384,128,128]{4,3,2,1,0:T(8,128)(2,1)}, u32[]{:S(2)}) copy-start(bf16[1,1,384,128,128]{4,3,2,1,0:T(8,128)(2,1)} %param.13) | copy-start | bytes 37748740
  36.1 171.3 %all-reduce.9.cloned.1.call-start = ((), (), s32[]{:S(2)}) async-start(), calls=%async_computation | async-start | bytes 4194304 | tf_op jit(solution)/shard_map/psum | solution.py:66
  113.1 3.3 copy-start.6
  116.3 91.1 %copy-start.1 = (f32[4096,128]{1,0:T(8,128)S(1)}, f32[4096,128]{1,0:T(8,128)}, u32[]{:S(2)}) copy-start(f32[4096,128]{1,0:T(8,128)} %param.17) | copy-start | bytes 6291460
  116.3 306.5 %all-reduce.11.cloned.1.call-start = ((), (), s32[]{:S(2)}) async-start(), calls=%async_computation.1 | async-start | bytes 2097152 | tf_op jit(solution)/shard_map/psum | solution.py:32
  362.5 60.4 %copy-start.2 = (f32[2048,128]{1,0:T(8,128)S(1)}, f32[2048,128]{1,0:T(8,128)}, u32[]{:S(2)}) copy-start(f32[2048,128]{1,0:T(8,128)} %get-tuple-element.70) | copy-start | bytes 3145732
  365.4 162.8 %all-reduce.13.cloned.1.call-start = ((), (), s32[]{:S(2)}) async-start(), calls=%async_computation.2 | async-start | bytes 4194304 | tf_op jit(solution)/shard_map/psum | solution.py:66
  437.4 308.9 %all-reduce.15.cloned.1.call-start = ((), (), s32[]{:S(2)}) async-start(), calls=%async_computation.3 | async-start | bytes 2097152 | tf_op jit(solution)/shard_map/psum | solution.py:32
  531.4 1.3 copy-start.4
  603.3 1.3 copy-start.3
  688.7 162.9 %all-reduce.17.cloned.1.call-start = ((), (), s32[]{:S(2)}) async-start(), calls=%async_computation.4 | async-start | bytes 4194304 | tf_op jit(solution)/shard_map/psum | solution.py:66
Sparse Core Ops, SparseCore 0:
  36.2 66.9 all-reduce.18
  116.5 90.8 all-reduce.8
  365.5 57.3 all-reduce.10
  437.5 90.6 all-reduce.12
  688.8 57.4 all-reduce.14
  760.9 90.6 all-reduce.16
where the time goes:
time: 1000 us; the launch traced here: 995 us
  blocking collectives  384 us (38%)
  waiting for transfers between devices  383 us (38%)
  other arithmetic  108 us (11%)
  matrix products  55.5 us (6%)
  local copies, waits for them, and re-layouts  41.8 us (4%)
  between operations  21.5 us (2%)
    psum x3, waiting for transfers between devices, on_device(): image = lax.psum(partial_feat, 'ex') + lam_part * direction  201 us
    psum x3, waiting for transfers between devices, forward(): return lax.psum(partial_rows, 'feat')  182 us
    psum x2, blocking collectives, on_device(): curv_sum = lax.psum(jnp.sum(own_dir * own_image), ('ex', 'feat'))  131 us
    psum x2, blocking collectives, on_device(): next_norm = lax.psum(jnp.sum(own_res * own_res), ('ex', 'feat'))  126 us
    psum x1, blocking collectives, on_device(): norm_now = lax.psum(jnp.sum(mine * mine), ('ex', 'feat'))  65.3 us
    psum x1, blocking collectives, on_device(): totals = lax.psum(jnp.sum(per_block, axis=0), ('ex', 'feat'))  62.6 us
    reduce_sum x16, other arithmetic, lookup(): return jnp.sum(jnp.where(matches, field_lambda, 0.0), axis=-1)  46.3 us
    dot_general x4, matrix products, forward(): jnp.einsum('tij,tj->ti', tile_stack, pieces, preferred_element_type=jnp.f...  36.4 us
  transfers between devices with their start and end apart: 6, of which 6 were waited for; matrix products, arithmetic and copies ran while one was open for 7% of the time, Pallas kernels for 0%

commit v1 on v0

--- a/solution.py
+++ b/solution.py
@@ -1,15 +1,491 @@
+import functools
 import math
 
 import jax
 import jax.numpy as jnp
 from jax import lax
+from jax.experimental import pallas as pl
+from jax.experimental.pallas import tpu as pltpu
 from jax.sharding import PartitionSpec as P
 
 RT_DEV = 2048
 ITERS = 3
-
-
-def on_device(tiles, row_index, col_index, weights, val_grad, field_map, field_lambda):
+CAP_ROW = 96
+CAP_COL = 64
+CHUNKS = 6
+GROUP = 16
+MESH = pl.DeviceIdType.MESH
+F32 = jnp.float32
+BF16 = jnp.bfloat16
+NN = (((1,), (0,)), ((), ()))
+NT = (((1,), (1,)), ((), ()))
+
+
+def iota(shape, axis):
+    return lax.broadcasted_iota(jnp.int32, shape, axis)
+
+
+def dot(a, b, dims=NN):
+    return lax.dot_general(a, b, dims, preferred_element_type=F32)
+
+
+def fold(x):
+    return jnp.sum(x.reshape(-1, 8, x.shape[-1]), axis=0)
+
+
+def one_hot(cond):
+    return jnp.where(cond, 1.0, 0.0).astype(BF16)
+
+
+def send_all(axis, src, dst, send_sem, recv_sem):
+    n = dst.shape[0]
+    me = lax.axis_index(axis)
+
+    def one(k, carry):
+        peer = lax.rem(me + k, n)
+        pltpu.make_async_remote_copy(
+            src_ref=src.at[peer], dst_ref=dst.at[me], send_sem=send_sem, recv_sem=recv_sem,
+            device_id={axis: peer}, device_id_type=MESH,
+        ).start()
+        return carry
+
+    lax.fori_loop(1, n, one, 0, unroll=True)
+    dst[me] = src[me]
+
+
+def share_all(axis, value, dst, send_sem, recv_sem):
+    n = dst.shape[0]
+    me = lax.axis_index(axis)
+    dst[me] = value
+
+    def one(k, carry):
+        peer = lax.rem(me + k, n)
+        pltpu.make_async_remote_copy(
+            src_ref=dst.at[me], dst_ref=dst.at[me], send_sem=send_sem, recv_sem=recv_sem,
+            device_id={axis: peer}, device_id_type=MESH,
+        ).start()
+        return carry
+
+    lax.fori_loop(1, n, one, 0, unroll=True)
+
+
+def drain(axis, dst, send_sem, recv_sem, sent):
+    n = dst.shape[0]
+    me = lax.axis_index(axis)
+    blocks = dst.at[pl.ds(0, n - 1)]
+    copy = pltpu.make_async_remote_copy(
+        src_ref=blocks, dst_ref=blocks, send_sem=send_sem, recv_sem=recv_sem,
+        device_id={axis: lax.rem(me + 1, n)}, device_id_type=MESH,
+    )
+    if sent:
+        copy.wait_send()
+    else:
+        copy.wait_recv()
+
+
+def slots(ids, shift, cap, n, s_ref, st_ref):
+    nt = ids.shape[1]
+    sq0, sq1 = iota((nt, nt), 0), iota((nt, nt), 1)
+    eye = sq0 == sq1
+    owner_l = (ids >> shift).astype(F32)
+    local_l = (ids & ((1 << shift) - 1)).astype(F32)
+    owner_s = jnp.sum(jnp.where(eye, owner_l, 0.0), axis=1, keepdims=True)
+    local_s = jnp.sum(jnp.where(eye, local_l, 0.0), axis=1, keepdims=True)
+    same = owner_s == owner_l
+    rank_s = jnp.sum(jnp.where(same & (sq1 < sq0), 1.0, 0.0), axis=1, keepdims=True)
+    rank_l = jnp.sum(jnp.where(same & (sq0 < sq1), 1.0, 0.0), axis=0, keepdims=True)
+    slot_s = jnp.where(rank_s < cap, owner_s * cap + rank_s, -1.0).astype(jnp.int32)
+    slot_l = jnp.where(rank_l < cap, owner_l * cap + rank_l, -1.0).astype(jnp.int32)
+    s_ref[...] = one_hot(iota((n * cap, nt), 0) == slot_l)
+    st_ref[...] = one_hot(iota((nt, n * cap), 1) == slot_s)
+    over = jnp.sum(jnp.where(rank_s < cap, 0.0, 1.0))
+    listed = jnp.broadcast_to(local_s + 1.0, (nt, 128)).astype(BF16)
+    return over, listed
+
+
+def tile_groups(count):
+    return count // GROUP
+
+
+def forward_group(tile_ref, base, lhs):
+    copies = lhs.shape[0] // GROUP
+    row = iota((GROUP, 128), 0)
+    accs = [jnp.zeros((GROUP, 128), F32)] * copies
+    for k in range(0, GROUP, 2):
+        pair = tile_ref[pl.ds(base + k, 2)].reshape(256, 128)
+        res = dot(lhs, pair, NT)
+        for c in range(copies):
+            part = res[c * GROUP:(c + 1) * GROUP]
+            accs[c] = jnp.where(row == k, part[:, :128], accs[c])
+            accs[c] = jnp.where(row == k + 1, part[:, 128:], accs[c])
+    return accs
+
+
+def forward(tile_ref, piece_ref, out_ref):
+    def group(g, carry):
+        base = pl.multiple_of(g * GROUP, GROUP)
+        (acc,) = forward_group(tile_ref, base, piece_ref[pl.ds(base, GROUP), :])
+        out_ref[pl.ds(base, GROUP), :] = acc.astype(out_ref.dtype)
+        return carry
+
+    lax.fori_loop(0, tile_groups(tile_ref.shape[0]), group, 0, unroll=8)
+
+
+def backward(tile_ref, piece_ref, out_ref):
+    row = iota((GROUP, 128), 0)
+    even = lax.rem(row, 2) == 0
+
+    def group(g, carry):
+        base = pl.multiple_of(g * GROUP, GROUP)
+        piece = piece_ref[pl.ds(base, GROUP), :]
+        zero = jnp.zeros_like(piece)
+        lhs = jnp.concatenate([jnp.where(even, piece, zero), jnp.where(even, zero, piece)], axis=1)
+        acc = jnp.zeros((GROUP, 128), F32)
+        for k in range(0, GROUP, 2):
+            pair = tile_ref[pl.ds(base + k, 2)].reshape(256, 128)
+            acc = jnp.where((row == k) | (row == k + 1), dot(lhs, pair), acc)
+        out_ref[pl.ds(base, GROUP), :] = acc.astype(out_ref.dtype)
+        return carry
+
+    lax.fori_loop(0, tile_groups(tile_ref.shape[0]), group, 0, unroll=8)
+
+
+def split(x):
+    high = x.astype(BF16)
+    return jnp.concatenate([high, (x - high.astype(F32)).astype(BF16)], axis=1)
+
+
+def halves(x):
+    return x[:, :128] + x[:, 128:]
+
+
+def kernel(
+    dims, row_ids, col_ids, col_smem, lam_smem, tiles_hbm, w_hbm, g_hbm, map_hbm,
+    sol_ref, hyp_ref,
+    tile, w_b, w_f, g_f, field, piece_w, piece_g, piece_a, prod,
+    s_r, st_r, s_c, st_c, m_r, mt_r, m_c, mt_c,
+    list_r, list_c, rlist_r, rlist_c,
+    part_0, rpart_0, part_r, rpart_r, part_c, rpart_c, gath_r, rgath_r, gath_c, rgath_c,
+    red_a, red_a2, red_s, red_s2, red_e, red_e2,
+    lam_own, fsum, fields,
+    tile_sem, load_sem, send_sem, recv_sem,
+):
+    nf, ne, nt, own, scale = dims
+    e_at = lax.axis_index("ex")
+
+    first = pl.multiple_of(e_at * own, own)
+    loads = [
+        pltpu.make_async_copy(g_hbm, g_f, load_sem.at[0]),
+        pltpu.make_async_copy(w_hbm, w_b, load_sem.at[1]),
+        pltpu.make_async_copy(map_hbm.at[pl.ds(first, own)], field, load_sem.at[2]),
+    ]
+    per = nt // CHUNKS
+    for c in range(CHUNKS):
+        loads.append(
+            pltpu.make_async_copy(
+                tiles_hbm.at[pl.ds(c * per, per)], tile.at[pl.ds(c * per, per)], tile_sem.at[c]
+            )
+        )
+    for copy in loads:
+        copy.start()
+    barrier = pltpu.get_barrier_semaphore()
+    for axis, n in (("feat", nf), ("ex", ne)):
+        me = lax.axis_index(axis)
+
+        def greet(k, carry, axis=axis, n=n, me=me):
+            pl.semaphore_signal(
+                barrier, inc=1, device_id={axis: lax.rem(me + k, n)}, device_id_type=MESH
+            )
+            return carry
+
+        lax.fori_loop(1, n, greet, 0, unroll=True)
+
+    sems = {}
+
+    def sem(name):
+        at = sems.setdefault(name, len(sems))
+        return send_sem.at[at], recv_sem.at[at]
+
+    pending = []
+
+    def post(axis, src, dst, name):
+        send_all(axis, src, dst, *sem(name))
+        pending.append((axis, dst, name))
+
+    def share(axis, value, dst, name):
+        share_all(axis, value, dst, *sem(name))
+        pending.append((axis, dst, name))
+
+    def arrive(axis, dst, name):
+        drain(axis, dst, *sem(name), False)
+
+    over_r, local_r = slots(row_ids[...], 8, CAP_ROW, nf, s_r, st_r)
+    over_c, local_c = slots(col_ids[...], 8, CAP_COL, ne, s_c, st_c)
+    list_r[...] = dot(s_r[...], local_r).astype(BF16).reshape(list_r.shape)
+    list_c[...] = dot(s_c[...], local_c).astype(BF16).reshape(list_c.shape)
+    pl.semaphore_wait(barrier, nf + ne - 2)
+    post("feat", list_r, rlist_r, "list_r")
+    post("ex", list_c, rlist_c, "list_c")
+
+    loads[0].wait()
+    loads[1].wait()
+    w_f[...] = w_b[...].astype(F32)
+
+    def fetch(t, carry):
+        at = col_smem[t]
+        piece_w[pl.ds(t, 1), :] = w_f[pl.ds(at, 1), :]
+        piece_g[pl.ds(t, 1), :] = g_f[pl.ds(at, 1), :]
+        return carry
+
+    lax.fori_loop(0, nt, fetch, 0, unroll=16)
+
+    def first_chunk(c):
+        def group(g, carry):
+            base = pl.multiple_of(c * per + g * GROUP, GROUP)
+            rows = pl.ds(base, GROUP)
+            lhs = jnp.concatenate(
+                [piece_w[rows, :].astype(BF16), piece_g[rows, :].astype(BF16)], axis=0
+            )
+            piece_w[rows, :], piece_g[rows, :] = forward_group(tile, base, lhs)
+            return carry
+
+        lax.fori_loop(0, tile_groups(per), group, 0, unroll=True)
+
+    for c in range(CHUNKS):
+        loads[3 + c].wait()
+        first_chunk(c)
+
+    def pack(s_ref, x, out):
+        out[...] = halves(dot(s_ref[...], split(x))).reshape(out.shape)
+
+    def unpack(m_ref, x):
+        return halves(dot(m_ref[...], split(x.reshape(-1, 128))))
+
+    sent_w = halves(dot(s_r[...], split(piece_w[...]))).reshape(nf, CAP_ROW, 128)
+    sent_g = halves(dot(s_r[...], split(piece_g[...]))).reshape(nf, CAP_ROW, 128)
+    part_0[:, 0] = sent_w
+    part_0[:, 1] = sent_g
+    post("feat", part_0, rpart_0, "part_0")
+
+    def owner_maps(axis, listed, name, mt_ref, m_ref):
+        arrive(axis, listed, name)
+        got = listed[...].reshape(-1, 128).astype(F32)
+        lane = iota(got.shape, 1).astype(F32)
+        for h in range(own // 128):
+            half = one_hot(got == lane + (1.0 + 128 * h))
+            mt_ref[:, 128 * h:128 * (h + 1)] = half
+            m_ref[128 * h:128 * (h + 1), :] = half.T
+
+    owner_maps("feat", rlist_r, "list_r", mt_r, m_r)
+    owner_maps("ex", rlist_c, "list_c", mt_c, m_c)
+    loads[2].wait()
+
+    def penalties(i, carry):
+        rows = pl.ds(pl.multiple_of(i * 32, 32), 32)
+        ids = field[rows, :]
+        acc = jnp.zeros(ids.shape, F32)
+        for k in range(64):
+            acc = jnp.where(ids == k, lam_smem[k], acc)
+        lam_own[rows, :] = acc
+        return carry
+
+    lax.fori_loop(0, own // 32, penalties, 0)
+    lam = lam_own[...]
+    mine = pl.ds(first, own)
+    weights = w_f[mine, :]
+    grad = g_f[mine, :]
+    fsum[...] = jnp.zeros_like(fsum)
+
+    def field_sums(x, at):
+        fields[...] = x * w_f[mine, :]
+
+        def one(k, carry):
+            fsum[pl.ds(k, 1), :] = jnp.sum(
+                fold(jnp.where(field[...] == k, fields[...], 0.0)), axis=0, keepdims=True
+            )
+            return carry
+
+        lax.fori_loop(0, 64, one, 0, unroll=4)
+        red_e_rows.append(jnp.sum(fsum[...].T, axis=0, keepdims=True))
+
+    red_e_rows = []
+    norm = fold(grad * grad)
+    field_sums(grad, 0)
+
+    arrive("feat", rpart_0, "part_0")
+    margin = unpack(m_r, rpart_0[:, 0])
+    prob = jax.nn.sigmoid(margin)
+    curv = prob * (1.0 - prob)
+    rows_sum = unpack(m_r, rpart_0[:, 1])
+    residual = grad
+    direction = grad
+    sol = jnp.zeros_like(grad)
+    beta = None
+    reduced = None
+
+    def total(x):
+        return jnp.sum(jnp.sum(x, axis=0, keepdims=True), axis=1, keepdims=True)
+
+    over = jnp.broadcast_to(over_r + over_c, (8, 128))
+    for step in range(ITERS):
+        tag = str(step)
+        if step:
+            arrive("feat", red_s2.at[2 * step - 2], "nn_f" + str(step - 1))
+            next_norm = total(jnp.sum(red_s2[2 * step - 2], axis=0))
+            beta = next_norm / norm_all
+            norm_all = next_norm
+            direction = residual + beta * direction
+            arrive("feat", rpart_r.at[step - 1], "part_r" + tag)
+            rows_sum = unpack(m_r, rpart_r[step - 1]) + beta * rows_sum
+        scaled_b = (curv * rows_sum).astype(BF16)
+        bend = fold(rows_sum * scaled_b.astype(F32)) + fold(lam * direction * direction)
+        if step + 1 == ITERS:
+            break
+        gath_r[step] = dot(mt_r[...], scaled_b).astype(BF16).reshape(nf, CAP_ROW, 128)
+        post("feat", gath_r.at[step], rgath_r.at[step], "gath_r" + tag)
+        if step == 0:
+            share("ex", jnp.concatenate([bend, norm, over], axis=0), red_a, "curv_e" + tag)
+        else:
+            share("ex", bend, red_s.at[2 * step - 1], "curv_e" + tag)
+
+        arrive("feat", rgath_r.at[step], "gath_r" + tag)
+        piece_a[...] = dot(st_r[...], rgath_r[step].reshape(-1, 128)).astype(BF16)
+        if step == 0:
+            arrive("ex", red_a, "curv_e" + tag)
+            share("feat", jnp.sum(red_a[...], axis=0), red_a2, "curv_f" + tag)
+        else:
+            arrive("ex", red_s.at[2 * step - 1], "curv_e" + tag)
+            share("feat", jnp.sum(red_s[2 * step - 1], axis=0), red_s2.at[2 * step - 1], "curv_f" + tag)
+        backward(tile, piece_a, prod)
+        pack(s_c, prod[...], part_c.at[step])
+        post("ex", part_c.at[step], rpart_c.at[step], "part_c" + tag)
+
+        if step == 0:
+            arrive("feat", red_a2, "curv_f" + tag)
+            both = jnp.sum(red_a2[...], axis=0)
+            norm_all = total(both[8:16])
+            over_all = both[16:24]
+            size = norm_all / total(both[:8])
+        else:
+            arrive("feat", red_s2.at[2 * step - 1], "curv_f" + tag)
+            size = norm_all / total(jnp.sum(red_s2[2 * step - 1], axis=0))
+        sol = sol + size * direction
+        arrive("ex", rpart_c.at[step], "part_c" + tag)
+        image = unpack(m_c, rpart_c[step]) + lam * direction
+        residual = residual - size * image
+        gath_c[step] = dot(mt_c[...], residual.astype(BF16)).astype(BF16).reshape(ne, CAP_COL, 128)
+        post("ex", gath_c.at[step], rgath_c.at[step], "gath_c" + tag)
+        share("ex", fold(residual * residual), red_s.at[2 * step], "nn_e" + tag)
+        field_sums(residual, step + 1)
+        arrive("ex", rgath_c.at[step], "gath_c" + tag)
+        piece_a[...] = dot(st_c[...], rgath_c[step].reshape(-1, 128)).astype(BF16)
+        arrive("ex", red_s.at[2 * step], "nn_e" + tag)
+        share("feat", jnp.sum(red_s[2 * step], axis=0), red_s2.at[2 * step], "nn_f" + tag)
+        forward(tile, piece_a, prod)
+        pack(s_r, prod[...], part_r.at[step])
+        post("feat", part_r.at[step], rpart_r.at[step], "part_r" + str(step + 1))
+        if step == 0:
+            betas = []
+            sizes = []
+        sizes.append(size)
+        if beta is not None:
+            betas.append(beta)
+    betas.append(beta)
+
+    pad = jnp.zeros((16 - 8 - ITERS, 128), F32)
+    share("ex", jnp.concatenate([bend] + red_e_rows + [pad], axis=0), red_e, "end_e")
+    arrive("ex", red_e, "end_e")
+    share("feat", jnp.sum(red_e[...], axis=0), red_e2, "end_f")
+    arrive("feat", red_e2, "end_f")
+    last = jnp.sum(red_e2[...], axis=0)
+    size = norm_all / total(last[:8])
+    sizes.append(size)
+    sol_ref[...] = sol + size * direction
+    by_dir = last[8:9]
+    per_field = sizes[0] * by_dir
+    for k in range(1, ITERS):
+        by_dir = last[8 + k:9 + k] + betas[k - 1] * by_dir
+        per_field = per_field + sizes[k] * by_dir
+    lane = iota((1, 128), 1)
+    lam_lane = jnp.zeros((1, 128), F32)
+    for k in range(64):
+        lam_lane = jnp.where(lane == k, lam_smem[k], lam_lane)
+    hyper = -lam_lane * per_field * scale
+    hyp_ref[...] = jnp.where(iota((8, 128), 0) == 0, jnp.broadcast_to(hyper, (8, 128)), over_all)
+    for axis, dst, name in pending:
+        drain(axis, dst, *sem(name), True)
+
+
+def fast(mesh_sizes, tiles, row_index, col_index, weights, val_grad, field_map, field_lambda):
+    nf, ne = mesh_sizes
+    nt, width = tiles.shape[2], tiles.shape[3]
+    segment = weights.shape[0]
+    own = segment // ne
+    scale = 1.0 / math.sqrt(segment * width * nf // field_lambda.shape[0])
+    sr, sc = nf * CAP_ROW, ne * CAP_COL
+    vmem, anyspace, smem = (
+        pl.BlockSpec(memory_space=pltpu.VMEM),
+        pl.BlockSpec(memory_space=pl.ANY),
+        pl.BlockSpec(memory_space=pltpu.SMEM),
+    )
+    steps = ITERS - 1
+    scratch = [
+        pltpu.VMEM((nt, width, width), BF16),
+        pltpu.VMEM((segment, width), BF16),
+        pltpu.VMEM((segment, width), F32),
+        pltpu.VMEM((segment, width), F32),
+        pltpu.VMEM((own, width), jnp.int32),
+        pltpu.VMEM((nt, width), F32),
+        pltpu.VMEM((nt, width), F32),
+        pltpu.VMEM((nt, width), BF16),
+        pltpu.VMEM((nt, width), F32),
+        pltpu.VMEM((sr, nt), BF16),
+        pltpu.VMEM((nt, sr), BF16),
+        pltpu.VMEM((sc, nt), BF16),
+        pltpu.VMEM((nt, sc), BF16),
+        pltpu.VMEM((own, sr), BF16),
+        pltpu.VMEM((sr, own), BF16),
+        pltpu.VMEM((own, sc), BF16),
+        pltpu.VMEM((sc, own), BF16),
+    ]
+    scratch += [pltpu.VMEM((nf, CAP_ROW, width), BF16), pltpu.VMEM((ne, CAP_COL, width), BF16)] * 2
+    scratch += [pltpu.VMEM((nf, 2, CAP_ROW, width), F32)] * 2
+    scratch += [pltpu.VMEM((steps, nf, CAP_ROW, width), F32)] * 2
+    scratch += [pltpu.VMEM((steps, ne, CAP_COL, width), F32)] * 2
+    scratch += [pltpu.VMEM((steps, nf, CAP_ROW, width), BF16)] * 2
+    scratch += [pltpu.VMEM((steps, ne, CAP_COL, width), BF16)] * 2
+    for rows in (24, None, 16):
+        lead = (4,) if rows is None else ()
+        scratch += [pltpu.VMEM(lead + (n, rows or 8, width), F32) for n in (ne, nf)]
+    scratch += [
+        pltpu.VMEM((own, width), F32),
+        pltpu.VMEM((width, width), F32),
+        pltpu.VMEM((own, width), F32),
+        pltpu.SemaphoreType.DMA((CHUNKS,)),
+        pltpu.SemaphoreType.DMA((3,)),
+        pltpu.SemaphoreType.DMA((24,)),
+        pltpu.SemaphoreType.DMA((24,)),
+    ]
+    cols = col_index.reshape(nt)
+    return pl.pallas_call(
+        functools.partial(kernel, (nf, ne, nt, own, scale)),
+        out_shape=(
+            jax.ShapeDtypeStruct((own, width), F32),
+            jax.ShapeDtypeStruct((8, width), F32),
+        ),
+        in_specs=[vmem, vmem, smem, smem, anyspace, anyspace, anyspace, anyspace],
+        out_specs=(vmem, vmem),
+        scratch_shapes=scratch,
+        compiler_params=pltpu.CompilerParams(
+            collective_id=0, has_side_effects=True, vmem_limit_bytes=52 << 20
+        ),
+    )(
+        row_index.reshape(1, nt), cols.reshape(1, nt), cols, field_lambda,
+        tiles.reshape(nt, width, width), weights, val_grad, field_map,
+    )
+
+
+def general(tiles, row_index, col_index, weights, val_grad, field_map, field_lambda):
     tile_count = tiles.shape[2]
     tile_width = tiles.shape[3]
     tile_stack = tiles.reshape(tile_count, tile_width, tile_width)
@@ -99,9 +575,19 @@
     return (own_solution, hypergrad)
 
 
+def on_device(mesh_sizes, *args):
+    own_solution, packed = fast(mesh_sizes, *args)
+    fields = args[-1].shape[0]
+    return lax.cond(
+        packed[1, 0] > 0.5,
+        lambda: general(*args),
+        lambda: (own_solution, packed[0, :fields]),
+    )
+
+
 def solution(mesh):
     return jax.shard_map(
-        on_device,
+        functools.partial(on_device, (mesh.shape["feat"], mesh.shape["ex"])),
         mesh=mesh,
         in_specs=(
             P("ex", "feat", None, None, None),

time: 1000 us -> 124 us (0.12)
  blocking collectives: 384 us -> 0 us
  waiting for transfers between devices: 383 us -> 0 us
  other arithmetic: 108 us -> 0.7 us
  Pallas kernels: 0 us -> 107 us
  matrix products: 55.5 us -> 0 us
  local copies, waits for them, and re-layouts: 41.8 us -> 1.2 us
    psum x6 -> x0, blocking collectives: 384 us -> none  [the longest x2 131 us: on_device(): curv_sum = lax.psum(jnp.sum(own_dir * own_image), ('ex', 'feat'))]
    psum x6 -> x0, waiting for transfers between devices: 383 us -> none  [the longest x3 201 us: on_device(): image = lax.psum(partial_feat, 'ex') + lam_part * direction]
    pallas_call x0 -> x1, Pallas kernels: none -> 107 us  [fast(): pl.pallas_call(functools.partial(kernel, (nf, ne, nt, own, scale)), out_s...]
    dot_general x7 -> x0, matrix products: 55.5 us -> none  [the longest x4 36.4 us: forward(): jnp.einsum('tij,tj->ti', tile_stack, pieces, preferred_element_type=jnp.f...]
    reduce_sum x22 -> x0, other arithmetic: 54.7 us -> none  [the longest x16 46.3 us: lookup(): return jnp.sum(jnp.where(matches, field_lambda, 0.0), axis=-1)]
    scatter-add x7 -> x0, other arithmetic: 21.3 us -> none  [the longest x4 11.4 us: forward(): jnp.zeros((RT_DEV, tile_width), jnp.float32).at[row_ids].add(products)]
    convert_element_type x6 -> x0, other arithmetic: 15.8 us -> none  [the longest x2 7.49 us: on_device(): dir_b = direction.astype(jnp.bfloat16)]
    eq x16 -> x0, local copies, waits for them, and re-layouts: 14.8 us -> none  [lookup(): matches = field_block[..., None] == labels]
  transfers between devices with their start and end apart: 6 -> 0, of which waited for: 6 -> 0; matrix products, arithmetic and copies ran while one was open for 7% -> 0% of each run, Pallas kernels for 0% -> 0%
where the time goes in v1:
time: 124 us
  Pallas kernels  107 us (86%)
  between operations  14.7 us (12%)
    pallas_call x1, Pallas kernels, fast(): pl.pallas_call(functools.partial(kernel, (nf, ne, nt, own, scale)), out_s...  107 us

profile of v1, /device:TPU:1, one launch (start us, length us, event | category | flops | bytes accessed | tf_op | source)
XLA Modules:
  0.0 124.1 jit_solution(4209905017387640884)
XLA Ops:
  7.2 0.7 reduce.4.col_smem
  7.9 0.0 copy-start.1
  7.9 0.0 copy-start.7
  7.9 0.0 copy-start.8
  7.9 0.0 copy-start.9
  7.9 107.3 %shard_map.88 = (f32[256,128]{1,0:T(8,128)S(1)}, f32[8,128]{1,0:T(8,128)S(1)}) custom-call(s32[1,384]{1,0:T(1,128)} %bitcast.77, s32[1,384]{1,0:T(1,128)} %bitcast.76, s32[384]{0:T(512)S(1)} %reduce.4.col_smem, f32[64]{0:T(128)} %lam_smem.1, bf16[384,128,128]{2,1,0:T(8,128)(2,1)} %bitcast.65, bf16[4096,128]{1,0:T(8,128)(2,1)} %w_hbm.1, f32[4096,128]{1,0:T(8,128)} %g_hbm.1, ...), custom_call_target="tpu_custom_call" | custom-call | tf_op jit(solution)/shard_map/pallas_call | solution.py:470
  115.2 0.5 slice.6
  116.3 0.0 copy-done.1
  116.3 0.0 copy-done.7
  116.4 0.0 copy-done.8
  116.4 0.0 copy-done.9
  116.4 0.2 conditional.1
  116.6 0.0 copy-start.10
  116.6 0.7 copy.58
  117.3 0.0 copy-done.10
  (1 shorter events, 0.0 us)
Async XLA Ops:
  7.9 108.5 %copy-start.1 = (f32[4096,128]{1,0:T(8,128)S(1)}, f32[4096,128]{1,0:T(8,128)}, u32[]{:S(2)}) copy-start(f32[4096,128]{1,0:T(8,128)} %g_hbm.1) | copy-start | bytes 6291460
  7.9 108.5 %copy-start.7 = (s32[1,1,384]{2,1,0:T(1,128)S(1)}, s32[1,1,384]{2,1,0:T(1,128)}, u32[]{:S(2)}) copy-start(s32[1,1,384]{2,1,0:T(1,128)} %param.17) | copy-start | bytes 4612
  7.9 108.5 %copy-start.8 = (f32[64]{0:T(128)S(1)}, f32[64]{0:T(128)}, u32[]{:S(2)}) copy-start(f32[64]{0:T(128)} %lam_smem.1) | copy-start | bytes 772
  7.9 108.5 %copy-start.9 = (s32[1,1,384]{2,1,0:T(1,128)S(1)}, s32[1,1,384]{2,1,0:T(1,128)}, u32[]{:S(2)}) copy-start(s32[1,1,384]{2,1,0:T(1,128)} %param.16) | copy-start | bytes 4612
  116.6 0.7 copy-start.10

commit v2 on v1

--- a/solution.py
+++ b/solution.py
@@ -16,6 +16,7 @@
 GROUP = 16
 MESH = pl.DeviceIdType.MESH
 F32 = jnp.float32
+LOG2E = 1.4426950408889634
 BF16 = jnp.bfloat16
 NN = (((1,), (0,)), ((), ()))
 NT = (((1,), (1,)), ((), ()))
@@ -94,11 +95,11 @@
     same = owner_s == owner_l
     rank_s = jnp.sum(jnp.where(same & (sq1 < sq0), 1.0, 0.0), axis=1, keepdims=True)
     rank_l = jnp.sum(jnp.where(same & (sq0 < sq1), 1.0, 0.0), axis=0, keepdims=True)
-    slot_s = jnp.where(rank_s < cap, owner_s * cap + rank_s, -1.0).astype(jnp.int32)
-    slot_l = jnp.where(rank_l < cap, owner_l * cap + rank_l, -1.0).astype(jnp.int32)
+    slot_s = jnp.where(rank_s < cap - 1, owner_s * cap + rank_s, -1.0).astype(jnp.int32)
+    slot_l = jnp.where(rank_l < cap - 1, owner_l * cap + rank_l, -1.0).astype(jnp.int32)
     s_ref[...] = one_hot(iota((n * cap, nt), 0) == slot_l)
     st_ref[...] = one_hot(iota((nt, n * cap), 1) == slot_s)
-    over = jnp.sum(jnp.where(rank_s < cap, 0.0, 1.0))
+    over = jnp.sum(jnp.where(rank_s < cap - 1, 0.0, 1.0))
     listed = jnp.broadcast_to(local_s + 1.0, (nt, 128)).astype(BF16)
     return over, listed
 
@@ -256,16 +257,27 @@
         first_chunk(c)
 
     def pack(s_ref, x, out):
-        out[...] = halves(dot(s_ref[...], split(x))).reshape(out.shape)
-
-    def unpack(m_ref, x):
+        count, cap, _ = out.shape
+        largest = jnp.max(jnp.max(jnp.abs(x), axis=0, keepdims=True), axis=1, keepdims=True)
+        exponent = jnp.ceil(jnp.log(jnp.maximum(largest, 1e-30)) * LOG2E)
+        exponent = jnp.minimum(jnp.maximum(exponent, -96.0), 120.0)
+        fixed = jnp.clip(x * jnp.exp2(15.0 - exponent), -32767.0, 32767.0)
+        slotted = halves(dot(s_ref[...], split(jnp.round(fixed)))).reshape(count, cap, 128)
+        filled = jnp.where(
+            iota((count, cap, 128), 1) == cap - 1, exponent.reshape(1, 1, 1), slotted
+        )
+        out[...] = filled.astype(jnp.int32).astype(jnp.int16)
+
+    def unpack(m_ref, got):
+        x = got[...].astype(jnp.int32).astype(F32)
+        cap = x.shape[1]
+        x = x * jnp.exp2(x[:, cap - 1:, :] - 15.0)
         return halves(dot(m_ref[...], split(x.reshape(-1, 128))))
 
-    sent_w = halves(dot(s_r[...], split(piece_w[...]))).reshape(nf, CAP_ROW, 128)
-    sent_g = halves(dot(s_r[...], split(piece_g[...]))).reshape(nf, CAP_ROW, 128)
-    part_0[:, 0] = sent_w
-    part_0[:, 1] = sent_g
-    post("feat", part_0, rpart_0, "part_0")
+    pack(s_r, piece_w[...], part_0.at[0])
+    pack(s_r, piece_g[...], part_0.at[1])
+    post("feat", part_0.at[0], rpart_0.at[0], "part_w")
+    post("feat", part_0.at[1], rpart_0.at[1], "part_g")
 
     def owner_maps(axis, listed, name, mt_ref, m_ref):
         arrive(axis, listed, name)
@@ -312,11 +324,12 @@
     norm = fold(grad * grad)
     field_sums(grad, 0)
 
-    arrive("feat", rpart_0, "part_0")
-    margin = unpack(m_r, rpart_0[:, 0])
+    arrive("feat", rpart_0.at[0], "part_w")
+    margin = unpack(m_r, rpart_0.at[0])
     prob = jax.nn.sigmoid(margin)
     curv = prob * (1.0 - prob)
-    rows_sum = unpack(m_r, rpart_0[:, 1])
+    arrive("feat", rpart_0.at[1], "part_g")
+    rows_sum = unpack(m_r, rpart_0.at[1])
     residual = grad
     direction = grad
     sol = jnp.zeros_like(grad)
@@ -336,7 +349,7 @@
             norm_all = next_norm
             direction = residual + beta * direction
             arrive("feat", rpart_r.at[step - 1], "part_r" + tag)
-            rows_sum = unpack(m_r, rpart_r[step - 1]) + beta * rows_sum
+            rows_sum = unpack(m_r, rpart_r.at[step - 1]) + beta * rows_sum
         scaled_b = (curv * rows_sum).astype(BF16)
         bend = fold(rows_sum * scaled_b.astype(F32)) + fold(lam * direction * direction)
         if step + 1 == ITERS:
@@ -371,7 +384,7 @@
             size = norm_all / total(jnp.sum(red_s2[2 * step - 1], axis=0))
         sol = sol + size * direction
         arrive("ex", rpart_c.at[step], "part_c" + tag)
-        image = unpack(m_c, rpart_c[step]) + lam * direction
+        image = unpack(m_c, rpart_c.at[step]) + lam * direction
         residual = residual - size * image
         gath_c[step] = dot(mt_c[...], residual.astype(BF16)).astype(BF16).reshape(ne, CAP_COL, 128)
         post("ex", gath_c.at[step], rgath_c.at[step], "gath_c" + tag)
@@ -449,9 +462,9 @@
         pltpu.VMEM((sc, own), BF16),
     ]
     scratch += [pltpu.VMEM((nf, CAP_ROW, width), BF16), pltpu.VMEM((ne, CAP_COL, width), BF16)] * 2
-    scratch += [pltpu.VMEM((nf, 2, CAP_ROW, width), F32)] * 2
-    scratch += [pltpu.VMEM((steps, nf, CAP_ROW, width), F32)] * 2
-    scratch += [pltpu.VMEM((steps, ne, CAP_COL, width), F32)] * 2
+    scratch += [pltpu.VMEM((2, nf, CAP_ROW, width), jnp.int16)] * 2
+    scratch += [pltpu.VMEM((steps, nf, CAP_ROW, width), jnp.int16)] * 2
+    scratch += [pltpu.VMEM((steps, ne, CAP_COL, width), jnp.int16)] * 2
     scratch += [pltpu.VMEM((steps, nf, CAP_ROW, width), BF16)] * 2
     scratch += [pltpu.VMEM((steps, ne, CAP_COL, width), BF16)] * 2
     for rows in (24, None, 16):
@@ -485,6 +498,22 @@
     )
 
 
+def ring_sum(x, axes):
+    for axis in axes:
+        n = lax.axis_size(axis)
+        me = lax.axis_index(axis)
+        around = [(i, (i + 1) % n) for i in range(n)]
+        terms = lax.dynamic_update_index_in_dim(jnp.zeros((n,) + x.shape, x.dtype), x, me, 0)
+
+        def hop(k, carry, axis=axis, n=n, me=me, around=around):
+            held, terms = carry
+            held = lax.ppermute(held, axis, around)
+            return held, lax.dynamic_update_index_in_dim(terms, held, lax.rem(me + n - k, n), 0)
+
+        x = jnp.sum(lax.fori_loop(1, n, hop, (x, terms))[1], axis=0)
+    return x
+
+
 def general(tiles, row_index, col_index, weights, val_grad, field_map, field_lambda):
     tile_count = tiles.shape[2]
     tile_width = tiles.shape[3]
@@ -505,7 +534,7 @@
         pieces = jnp.take(vec_b, col_ids, axis=0)
         products = jnp.einsum("tij,tj->ti", tile_stack, pieces, preferred_element_type=jnp.float32)
         partial_rows = jnp.zeros((RT_DEV, tile_width), jnp.float32).at[row_ids].add(products)
-        return lax.psum(partial_rows, "feat")
+        return ring_sum(partial_rows, ("feat",))
 
     def lookup(field_block):
         matches = field_block[..., None] == labels
@@ -528,7 +557,7 @@
     solution = jnp.zeros_like(residual)
     dir_b = val_grad.astype(jnp.bfloat16)
     mine = local(residual)
-    norm_now = lax.psum(jnp.sum(mine * mine), ("ex", "feat"))
+    norm_now = ring_sum(jnp.sum(mine * mine), ("ex", "feat"))
     for step in range(ITERS):
         rows_sum = forward(dir_b)
         scaled_part = (curv_weight * rows_sum).astype(jnp.bfloat16)
@@ -539,16 +568,16 @@
         partial_feat = (
             jnp.zeros((segment, tile_width), jnp.float32).at[col_ids].add(backward_products)
         )
-        image = lax.psum(partial_feat, "ex") + lam_part * direction
+        image = ring_sum(partial_feat, ("ex",)) + lam_part * direction
         own_dir = local(direction)
         own_image = local(image)
-        curv_sum = lax.psum(jnp.sum(own_dir * own_image), ("ex", "feat"))
+        curv_sum = ring_sum(jnp.sum(own_dir * own_image), ("ex", "feat"))
         step_size = norm_now / curv_sum
         solution = solution + step_size * direction
         residual = residual - step_size * image
         if step + 1 < ITERS:
             own_res = local(residual)
-            next_norm = lax.psum(jnp.sum(own_res * own_res), ("ex", "feat"))
+            next_norm = ring_sum(jnp.sum(own_res * own_res), ("ex", "feat"))
         if step + 1 < ITERS:
             direction = residual + next_norm / norm_now * direction
             norm_now = next_norm
@@ -570,7 +599,7 @@
             own_fields.reshape(-1, share_block, tile_width),
         ),
     )
-    totals = lax.psum(jnp.sum(per_block, axis=0), ("ex", "feat"))
+    totals = ring_sum(jnp.sum(per_block, axis=0), ("ex", "feat"))
     hypergrad = -field_lambda * totals * norm_scale
     return (own_solution, hypergrad)
 

time: 124 us -> 99.7 us (0.80)
  between operations: 14.7 us -> 1.37 us
  Pallas kernels: 107 us -> 95.1 us
    pallas_call x1, Pallas kernels: 107 us -> 95.1 us  [fast(): pl.pallas_call(functools.partial(kernel, (nf, ne, nt, own, scale)), out_s...]
where the time goes in v2:
time: 99.7 us; the launch traced here: 99.5 us
  Pallas kernels  95.1 us (95%)
  local copies, waits for them, and re-layouts  2.11 us (2%)
  between operations  1.37 us (1%)
    pallas_call x1, Pallas kernels, fast(): pl.pallas_call(functools.partial(kernel, (nf, ne, nt, own, scale)), out_s...  95.1 us

profile of v2, /device:TPU:1, one launch (start us, length us, event | category | flops | bytes accessed | tf_op | source)
XLA Modules:
  0.0 99.5 jit_solution(12929205988234829769)
XLA Ops:
  0.6 0.7 reduce.4.col_smem
  1.3 0.0 copy-start
  1.3 0.0 copy-start.7
  1.3 0.0 copy-start.8
  1.4 0.0 copy-start.9
  1.4 95.1 %shard_map.88 = (f32[256,128]{1,0:T(8,128)}, f32[8,128]{1,0:T(8,128)S(1)}) custom-call(s32[1,384]{1,0:T(1,128)} %bitcast.175, s32[1,384]{1,0:T(1,128)} %bitcast.174, s32[384]{0:T(512)S(1)} %reduce.4.col_smem, f32[64]{0:T(128)} %lam_smem.1, bf16[384,128,128]{2,1,0:T(8,128)(2,1)} %bitcast.163, bf16[4096,128]{1,0:T(8,128)(2,1)} %w_hbm.1, f32[4096,128]{1,0:T(8,128)} %g_hbm.1, ...), custom_call_target="tpu_custom_call" | custom-call | tf_op jit(solution)/shard_map/pallas_call | solution.py:483
  96.5 0.5 slice.6
  97.6 0.0 copy-done
  97.6 0.0 copy-done.7
  97.6 0.0 copy-done.8
  97.7 0.0 copy-done.9
  97.7 0.2 conditional.1
  97.9 0.0 copy-start.10
  97.9 1.6 %copy.310 = f32[256,128]{1,0:T(8,128)} copy(f32[256,128]{1,0:T(8,128)} %get-tuple-element.3602) | data formatting | bytes 262144
  99.5 0.0 copy-done.10
  (1 shorter events, 0.0 us)
Async XLA Ops:
  1.3 96.3 %copy-start = (f32[4096,128]{1,0:T(8,128)S(1)}, f32[4096,128]{1,0:T(8,128)}, u32[]{:S(2)}) copy-start(f32[4096,128]{1,0:T(8,128)} %g_hbm.1) | copy-start | bytes 6291460
  1.3 96.3 %copy-start.7 = (s32[1,1,384]{2,1,0:T(1,128)S(1)}, s32[1,1,384]{2,1,0:T(1,128)}, u32[]{:S(2)}) copy-start(s32[1,1,384]{2,1,0:T(1,128)} %param.59) | copy-start | bytes 4612
  1.3 96.3 %copy-start.8 = (f32[64]{0:T(128)S(1)}, f32[64]{0:T(128)}, u32[]{:S(2)}) copy-start(f32[64]{0:T(128)} %lam_smem.1) | copy-start | bytes 772
  1.4 96.3 %copy-start.9 = (s32[1,1,384]{2,1,0:T(1,128)S(1)}, s32[1,1,384]{2,1,0:T(1,128)}, u32[]{:S(2)}) copy-start(s32[1,1,384]{2,1,0:T(1,128)} %param.58) | copy-start | bytes 4612
  97.9 1.6 %copy-start.10 = (f32[64]{0:T(128)}, f32[64]{0:T(128)S(1)}, u32[]{:S(2)}) copy-start(f32[64]{0:T(128)S(1)} %get-tuple-element.3603) | copy-start | bytes 772
